TPU v7x, 512 devices: a whole 4x8x8 slice. The times are simulated.
512 devices in a mesh: dp: 4 (over x_hi, core), context: 16 (over x_lo, z), tensor: 8 (over y).
Axes of the slice: x: 4 (x_hi: 2, x_lo: 2; x = x_hi * 2 + x_lo), y: 8, z: 8, core: 2. Of those that a mesh axis runs over, the one named last changes fastest.
Arguments:
- tokens: bfloat16 [32768, 4096], P(('dp', 'context', 'tensor')), parts along dimension 0, may hold values from -6 to 6
- norm_gain: bfloat16 [4096], replicated, may hold values from 0.099609375 to 1.8984375
- w_query: bfloat16 [4096, 2048], P(None, 'tensor'), may hold values from -2.03125 to 2.03125
- key_matrix: bfloat16 [4096, 1024], P(None, 'tensor'), may hold values from -0.109375 to 0.109375
- value_matrix: bfloat16 [4096, 1024], P(None, 'tensor'), may hold values from -0.09375 to 0.09375
- seg_ids: int32 [32768], P('dp'), parts along dimension 0, may hold values from 0 to 7, never falling along the last dimension, each value on 1 to 4096 neighbouring positions
Outputs:
- attended: bfloat16 [32768, 2048], P(('dp', 'context'), 'tensor'), parts along dimension 0
There are 4 independent parts, one for each index of `dp`. A program takes and returns all parts, laid end to end along the dimension named above; an argument that names none is the same for every part. Nothing has to cross between parts.
Inputs may be any that keep to these rules, and one draw needn't show every extreme that they name: `seg_ids`: never falls along the row; each of the 8 documents covers 1 to 4096 positions, one exactly 4096.
All inputs are finite; a program needn't handle non-finite values.
Results may differ from a plain program's by a relative error of at most 0.0078.
Values may be sent and summed in bfloat16 or wider, within the bound.
A program may use at most 64 MiB of HBM per device.

v0:
```python
import math
import jax
import jax.numpy as jnp
from jax import lax
from jax.sharding import PartitionSpec as P

HEAD_SIZE = 128


def sent_together(arrays, axis, dim, along):
    widths = [a.shape[along] for a in arrays]
    both = jnp.concatenate(arrays, axis=along)
    filled = lax.all_gather(both, axis, axis=dim, tiled=True)
    return tuple(jnp.split(filled, [sum(widths[:k]) for k in range(1, len(widths))], axis=along))


def rotate(vectors, positions):
    half_width = vectors.shape[-1] // 2
    inv_freq = jnp.exp(
        -(jnp.arange(half_width, dtype=jnp.float32) * (2.0 / vectors.shape[-1]))
        * math.log(500000.0)
    )
    angles = positions.astype(jnp.float32)[:, None] * inv_freq[None, :]
    cosine = jnp.cos(angles)[:, None, :]
    sine = jnp.sin(angles)[:, None, :]
    front_half = vectors[..., :half_width]
    back_half = vectors[..., half_width:]
    return jnp.concatenate(
        [front_half * cosine - back_half * sine, back_half * cosine + front_half * sine], -1
    )


def merge_block(
    states_in, query_heads, query_pos, query_segs, key_part, val_part, key_segs, key_pos
):
    peak_old, totals, weighted = states_in
    scores = jnp.einsum(
        "qkgd,skd->kgqs", query_heads, key_part, preferred_element_type=jnp.float32
    ) * (1.0 / math.sqrt(HEAD_SIZE))
    visible = (key_pos[None, :] <= query_pos[:, None]) & (key_segs[None, :] == query_segs[:, None])
    scores = jnp.where(visible[None, None], scores, -1e30)
    peak_new = jnp.maximum(peak_old, jnp.max(scores, -1))
    probs = jnp.where(visible[None, None], jnp.exp(scores - peak_new[..., None]), 0.0)
    rescale = jnp.exp(peak_old - peak_new)
    totals = totals * rescale + jnp.sum(probs, -1)
    weighted = weighted * rescale[..., None] + jnp.einsum(
        "kgqs,skd->kgqd", probs.astype(jnp.bfloat16), val_part, preferred_element_type=jnp.float32
    )
    return (peak_new, totals, weighted)


def body(tokens, norm_gain, w_query, key_matrix, value_matrix, seg_ids):
    wide_tokens = tokens.astype(jnp.float32)
    rms_normalized = (
        wide_tokens
        * lax.rsqrt(jnp.mean(wide_tokens * wide_tokens, -1, keepdims=True) + 1e-05)
        * norm_gain.astype(jnp.float32)
    ).astype(jnp.bfloat16)
    pieces = lax.all_gather(rms_normalized, "tensor", axis=0, tiled=True)
    projected = jnp.concatenate(
        [
            jnp.dot(pieces, w_query, preferred_element_type=jnp.float32),
            jnp.dot(pieces, key_matrix, preferred_element_type=jnp.float32),
            jnp.dot(pieces, value_matrix, preferred_element_type=jnp.float32),
        ],
        1,
    )
    span_rows = projected.shape[0]
    width_q = w_query.shape[1]
    width_k = key_matrix.shape[1]
    heads_q = width_q // HEAD_SIZE
    heads_kv = width_k // HEAD_SIZE
    heads_per_group = heads_q // heads_kv
    offset = lax.axis_index("context") * span_rows
    positions = offset + jnp.arange(span_rows, dtype=jnp.int32)
    query = rotate(projected[:, :width_q].reshape(span_rows, heads_q, HEAD_SIZE), positions).astype(
        jnp.bfloat16
    )
    key = rotate(
        projected[:, width_q : width_q + width_k].reshape(span_rows, heads_kv, HEAD_SIZE), positions
    ).astype(jnp.bfloat16)
    key = key.reshape(span_rows, width_k)
    value_rows = projected[:, width_q + width_k :].astype(jnp.bfloat16)
    groups = (query, positions, lax.dynamic_slice_in_dim(seg_ids, offset, span_rows, 0))
    query_rows, query_pos, query_segs = groups
    count = query_rows.shape[0]
    prepared = [
        (query_rows.reshape(count, heads_kv, heads_per_group, HEAD_SIZE), query_pos, query_segs)
    ]
    initial = [
        (
            jnp.full((heads_kv, heads_per_group, count), -1e30, jnp.float32),
            jnp.zeros((heads_kv, heads_per_group, count), jnp.float32),
            jnp.zeros((heads_kv, heads_per_group, count, HEAD_SIZE), jnp.float32),
        )
    ]
    states = tuple(initial)
    anchor = jnp.int32(0)
    keys_in, values_in = sent_together((key, value_rows), "context", 0, 1)
    length = keys_in.shape[0]
    sub_rows = math.gcd(length, 512)
    parts_count = length // sub_rows
    key_blocks = keys_in.reshape(parts_count, sub_rows, heads_kv, HEAD_SIZE)
    value_blocks = values_in.reshape(parts_count, sub_rows, heads_kv, HEAD_SIZE)
    key_pos_all = jnp.arange(length, dtype=jnp.int32)
    seg_blocks = seg_ids.reshape(parts_count, sub_rows)
    pos_blocks = key_pos_all.reshape(parts_count, sub_rows)
    results = []
    for (query_heads, query_pos, query_segs), states_in in zip(prepared, states):
        skipped = (anchor > jnp.max(query_pos)) | (seg_ids[length - 1] < jnp.min(query_segs))

        def update(carried, query_heads=query_heads, query_pos=query_pos, query_segs=query_segs):

            def inner(running, slices):
                key_part, val_part, key_segs, key_pos = slices
                return (
                    merge_block(
                        running,
                        query_heads,
                        query_pos,
                        query_segs,
                        key_part,
                        val_part,
                        key_segs,
                        key_pos,
                    ),
                    None,
                )

            return lax.scan(inner, carried, (key_blocks, value_blocks, seg_blocks, pos_blocks))[0]

        results.append(lax.cond(skipped, lambda carried: carried, update, states_in))
    finals = tuple(results)
    outputs = []
    for peak_val, totals, weighted in finals:
        count = weighted.shape[2]
        normalized = weighted / totals[..., None]
        outputs.append(
            jnp.transpose(normalized, (2, 0, 1, 3)).reshape(count, width_q).astype(jnp.bfloat16)
        )
    return outputs[0]


def solution(mesh):
    in_specs = (
        P(("dp", "context", "tensor"), None),
        P(),
        P(None, "tensor"),
        P(None, "tensor"),
        P(None, "tensor"),
        P("dp"),
    )
    out_specs = P(("dp", "context"), "tensor")
    return jax.shard_map(body, mesh=mesh, in_specs=in_specs, out_specs=out_specs, check_vma=False)
```

profile of v0, /device:TPU:8, one launch (start us, length us, event | category | flops | bytes accessed | tf_op | source)
XLA Modules:
  0.0 281.3 jit_solution(2508843274565658553)
XLA Ops:
  10.8 60.4 %all-gather.3.cloned.1.call-done = bf16[512,4096]{1,0:T(8,128)(2,1)} async-done(((bf16[64,4096]{1,0:T(8,128)(2,1)}), bf16[512,4096]{1,0:T(8,128)(2,1)}) %all-gather.3.cloned.1.call-update) | async-done | bytes 4194320 | tf_op jit(solution)/shard_map/all_gather | solution.py:59
  71.2 4.1 %convolution_bitcast_fusion.1 = f32[512,1,128]{0,2,1:T(8,128)S(1)} fusion(bf16[512,4096]{1,0:T(8,128)(2,1)} %all-gather.3.cloned.1.call-done, bf16[4096,128]{1,0:T(8,128)(2,1)} %param.13), kind=kOutput, calls=%fused_computation.37 | convolution fusion | flops 536870912 | bytes 5505024 | tf_op jit(solution)/shard_map/dot_general | solution.py:63
  84.1 3.5 %fusion.44 = f32[512,256]{0,1:T(8,128)S(1)} fusion(bf16[512,4096]{1,0:T(8,128)(2,1)} %all-gather.3.cloned.1.call-done, bf16[4096,256]{1,0:T(8,128)(2,1)S(1)} %copy-done), kind=kOutput, calls=%fused_computation.73 | convolution fusion | flops 1073741824 | bytes 6815744 | tf_op jit(solution)/shard_map/dot_general | solution.py:62
  89.4 69.8 %all-gather.5.cloned.1.call-done = bf16[8192,256]{0,1:T(8,128)(2,1)} async-done(((bf16[512,256]{0,1:T(8,128)(2,1)}), bf16[8192,256]{0,1:T(8,128)(2,1)}) %all-gather.5.cloned.1.call-update) | async-done | bytes 4194320 | tf_op jit(solution)/shard_map/all_gather | solution.py:13
  159.2 114.0 %conditional.1 = (f32[1,2,512]{2,1,0:T(2,128)S(1)}, f32[1,2,512,128]{3,2,1,0:T(8,128)S(1)}) conditional(s32[]{:T(128)} %convert_element_type.47, (bf16[8192,256]{0,1:T(8,128)(2,1)}, s32[8192]{0:T(1024)S(1)}, s32[16,512]{1,0:T(8,128)S(1)}, s32[16,512]{1,0:T(8,128)S(1)}, s32[512]{0:T(512)S(1)}, /*index=5*/s32[512]{0:T(512)S(1)}, ...), branch_computations={%region_3.8_spmd, %region_8.9_spmd} | conditional | flops 276453376 | bytes 34325800 | solution.py:132
  159.2 6.4 %copy.10 = bf16[8192,256]{1,0:T(8,128)(2,1)} copy(bf16[8192,256]{0,1:T(8,128)(2,1)} %get-tuple-element.134) | data formatting | bytes 8388608 | tf_op jit(solution)/shard_map
  165.6 4.5 %fusion.42 = (bf16[8192,128]{1,0:T(8,128)(2,1)}, bf16[8192,128]{1,0:T(8,128)(2,1)}) fusion(bf16[8192,256]{1,0:T(8,128)(2,1)} %copy.10), kind=kLoop, calls=%fused_computation.71 | loop fusion | bytes 8388608 | tf_op jit(solution)/shard_map/split | solution.py:14
  170.1 103.1 %while.14 = (s32[]{:T(128)}, f32[1,2,512]{2,1,0:T(2,128)S(1)}, f32[1,2,512]{2,1,0:T(2,128)S(1)}, f32[1,2,512,128]{3,2,1,0:T(8,128)S(1)}, s32[16,512]{1,0:T(8,128...) while((s32[]{:T(128)}, f32[1,2,512]{2,1,0:T(2,128)S(1)}, ...), condition=%wide.region_7.7_spmd.clone, body=%wide.region_4.6_spmd.clone.sunk | while | flops 276436992 | bytes 17384616 | solution.py:130
  170.4 2.8 fusion.59
  176.9 2.8 fusion.59
  183.3 2.8 fusion.59
  189.8 2.8 fusion.59
  196.2 2.8 fusion.59
  202.6 2.8 fusion.59
  209.1 2.8 fusion.59
  215.5 2.8 fusion.59
  222.0 2.8 fusion.59
  228.4 2.8 fusion.59
  234.9 2.8 fusion.59
  241.3 2.8 fusion.59
  247.7 2.8 fusion.59
  254.2 2.8 fusion.59
  260.6 2.8 fusion.59
  267.1 2.8 fusion.59
  (185 shorter events, 71.6 us)
Async XLA Ops:
  6.5 77.6 %copy-start = (bf16[4096,256]{1,0:T(8,128)(2,1)S(1)}, bf16[4096,256]{1,0:T(8,128)(2,1)}, u32[]{:S(2)}) copy-start(bf16[4096,256]{1,0:T(8,128)(2,1)} %param.12) | copy-start | bytes 6291460
  6.5 64.7 %all-gather.3.cloned.1.call-start = ((), (), s32[]{:S(2)}) async-start(), calls=%async_computation | async-start | bytes 4718592 | tf_op jit(solution)/shard_map/all_gather | solution.py:59
  10.7 148.5 %all-gather.5.cloned.1.call-start = ((), (), s32[]{:S(2)}) async-start(), calls=%async_computation.1 | async-start | bytes 4456448 | tf_op jit(solution)/shard_map/all_gather | solution.py:13
  10.8 65.1 %copy-start.3 = (bf16[4096,128]{1,0:T(8,128)(2,1)S(1)}, bf16[4096,128]{1,0:T(8,128)(2,1)}, u32[]{:S(2)}) copy-start(bf16[4096,128]{1,0:T(8,128)(2,1)} %param.14) | copy-start | bytes 3145732
  71.2 4.7 %copy-start.2 = (bf16[512,4096]{1,0:T(8,128)(2,1)S(1)}, bf16[512,4096]{1,0:T(8,128)(2,1)}, u32[]{:S(2)}) copy-start(bf16[512,4096]{1,0:T(8,128)(2,1)} %all-gather.3.cloned.1.call-done) | copy-start | bytes 12582916
  75.9 3.0 %copy-start.4 = (s32[8192]{0:T(1024)S(1)}, s32[8192]{0:T(1024)}, u32[]{:S(2)}) copy-start(s32[8192]{0:T(1024)} %param.15) | copy-start | bytes 98308
  173.2 2.7 copy-start.1
  179.7 2.7 copy-start.1
  186.1 2.7 copy-start.1
  192.6 2.7 copy-start.1
  199.0 2.7 copy-start.1
  205.4 2.7 copy-start.1
  211.9 2.7 copy-start.1
  218.3 2.7 copy-start.1
  224.8 2.7 copy-start.1
  231.2 2.7 copy-start.1
  237.6 2.7 copy-start.1
  244.1 2.7 copy-start.1
  250.5 2.7 copy-start.1
  257.0 2.7 copy-start.1
  263.4 2.7 copy-start.1
  269.9 2.7 copy-start.1
Sparse Core Ops, SparseCore 0:
  10.8 60.3 all-gather.2
  78.3 80.8 all-gather.4
where the time goes:
time: 282 us; the launch traced here: 281 us
  waiting for transfers between devices  130 us (46%)
  matrix products  96.7 us (34%)
  other arithmetic  24.4 us (9%)
  between operations  15.6 us (6%)
  local copies, waits for them, and re-layouts  13.3 us (5%)
    all_gather x1, waiting for transfers between devices, sent_together(): filled = lax.all_gather(both, axis, axis=dim, tiled=True)  69.8 us
    all_gather x1, waiting for transfers between devices, body(): pieces = lax.all_gather(rms_normalized, 'tensor', axis=0, tiled=True)  60.4 us
    dot_general x16, matrix products, merge_block(): jnp.einsum('qkgd,skd->kgqs', query_heads, key_part, preferred_element_typ...  44.4 us
    dot_general x16, matrix products, merge_block(): jnp.einsum('kgqs,skd->kgqd', probs.astype(jnp.bfloat16), val_part, prefer...  43.2 us
    reduce_sum x16, other arithmetic, merge_block(): totals = totals * rescale + jnp.sum(probs, -1)  9.2 us
    another operation x1, local copies, waits for them, and re-layouts  6.43 us
  transfers between devices with their start and end apart: 2, of which 2 were waited for; matrix products, arithmetic and copies ran while one was open for 3% of the time, Pallas kernels for 0%

commit v1 on v0

--- a/solution.py
+++ b/solution.py
@@ -56,7 +56,10 @@
         * lax.rsqrt(jnp.mean(wide_tokens * wide_tokens, -1, keepdims=True) + 1e-05)
         * norm_gain.astype(jnp.float32)
     ).astype(jnp.bfloat16)
-    pieces = lax.all_gather(rms_normalized, "tensor", axis=0, tiled=True)
+    pieces = jnp.concatenate(
+        lax.all_to_all(jnp.stack([rms_normalized] * lax.axis_size("tensor")), "tensor", 0, 0),
+        axis=0,
+    )
     projected = jnp.concatenate(
         [
             jnp.dot(pieces, w_query, preferred_element_type=jnp.float32),

time: 282 us -> 311 us (1.10)
  waiting for transfers between devices: 130 us -> 162 us
  matrix products: 96.7 us -> 81.5 us
  starting transfers between devices: 0.04 us -> 10.3 us
  local copies, waits for them, and re-layouts: 13.3 us -> 18.9 us
    all_to_all x0 -> x1, waiting for transfers between devices: none -> 92.1 us  [body(): lax.all_to_all(jnp.stack([rms_normalized] * lax.axis_size('tensor')), 'te...]
    all_gather x1 -> x0, waiting for transfers between devices: 60.4 us -> none  [body(): pieces = lax.all_gather(rms_normalized, 'tensor', axis=0, tiled=True)]
    dot_general x16, matrix products: 44.4 us -> 25.2 us  [merge_block(): jnp.einsum('qkgd,skd->kgqs', query_heads, key_part, preferred_element_typ...]
    all_to_all x0 -> x1, starting transfers between devices: none -> 10.3 us  [body(): lax.all_to_all(jnp.stack([rms_normalized] * lax.axis_size('tensor')), 'te...]
    another operation x1 -> x3, local copies, waits for them, and re-layouts: 6.43 us -> 9.74 us
where the time goes in v1:
time: 311 us; the launch traced here: 310 us
  waiting for transfers between devices  162 us (52%)
  matrix products  81.5 us (26%)
  other arithmetic  21.8 us (7%)
  local copies, waits for them, and re-layouts  18.9 us (6%)
  between operations  15.3 us (5%)
  starting transfers between devices  10.3 us (3%)
    all_to_all x1, waiting for transfers between devices, body(): lax.all_to_all(jnp.stack([rms_normalized] * lax.axis_size('tensor')), 'te...  92.1 us
    all_gather x1, waiting for transfers between devices, sent_together(): filled = lax.all_gather(both, axis, axis=dim, tiled=True)  69.5 us
    dot_general x16, matrix products, merge_block(): jnp.einsum('kgqs,skd->kgqd', probs.astype(jnp.bfloat16), val_part, prefer...  44.5 us
    dot_general x16, matrix products, merge_block(): jnp.einsum('qkgd,skd->kgqs', query_heads, key_part, preferred_element_typ...  25.2 us
    all_to_all x1, starting transfers between devices, body(): lax.all_to_all(jnp.stack([rms_normalized] * lax.axis_size('tensor')), 'te...  10.3 us
    reduce_sum x16, other arithmetic, merge_block(): totals = totals * rescale + jnp.sum(probs, -1)  9.06 us
    another operation x2, local copies, waits for them, and re-layouts  7.27 us
  transfers between devices with their start and end apart: 2, of which 2 were waited for; matrix products, arithmetic and copies ran while one was open for 3% of the time, Pallas kernels for 0%

profile of v1, /device:TPU:8, one launch (start us, length us, event | category | flops | bytes accessed | tf_op | source)
XLA Modules:
  0.0 310.3 jit_solution(12956365477695012744)
XLA Ops:
  12.3 10.3 %all-to-all-start = ((bf16[8,64,4096]{2,1,0:T(8,128)(2,1)}), bf16[8,64,4096]{2,1,0:T(8,128)(2,1)}, u32[]{:S(2)}, u32[]{:S(2)}) async-start(bf16[8,64,4096]{2,1,0:T(8,128)(2,1)} %stack.2), calls=%async_computation | async-start | bytes 8388608 | tf_op jit(solution)/shard_map/all_to_all | solution.py:60
  22.6 92.1 %all-to-all-done = bf16[8,64,4096]{2,1,0:T(8,128)(2,1)} async-done(((bf16[8,64,4096]{2,1,0:T(8,128)(2,1)}), bf16[8,64,4096]{2,1,0:T(8,128)(2,1)}, u32[]{:S(2)}, u32[]{:S(2)}) %all-to-all-start) | async-done | bytes 4194336 | tf_op jit(solution)/shard_map/all_to_all | solution.py:60
  114.6 3.8 %convolution_bitcast_fusion.1 = f32[512,1,128]{0,2,1:T(8,128)S(1)} fusion(bf16[512,4096]{1,0:T(8,128)(2,1)} %bitcast.3, bf16[4096,128]{1,0:T(8,128)(2,1)S(1)} %copy-done), kind=kOutput, calls=%fused_computation.37 | convolution fusion | flops 536870912 | bytes 5505024 | tf_op jit(solution)/shard_map/dot_general | solution.py:66
  118.4 3.8 %convolution_convert_fusion = bf16[512,128]{0,1:T(8,128)(2,1)S(1)} fusion(bf16[512,4096]{1,0:T(8,128)(2,1)} %bitcast.3, bf16[4096,128]{1,0:T(8,128)(2,1)S(1)} %copy-done.2), kind=kOutput, calls=%fused_computation.38 | convolution fusion | flops 536936448 | bytes 5373952 | tf_op jit(solution)/shard_map/dot_general | solution.py:67
  124.3 2.9 copy.13
  130.8 4.2 %fusion.43 = f32[512,2,128]{0,2,1:T(8,128)S(1)} fusion(bf16[512,4096,1]{1,0,2:T(8,128)(2,1)} %bitcast.7, bf16[2,128,4096]{2,1,0:T(8,128)(2,1)} %bitcast.110), kind=kOutput, calls=%fused_computation.72 | convolution fusion | flops 1073741824 | bytes 6815744 | tf_op jit(solution)/shard_map/dot_general | solution.py:65
  135.1 69.5 %all-gather.2.cloned.1.call-done = bf16[8192,256]{0,1:T(8,128)(2,1)} async-done(((bf16[512,256]{0,1:T(8,128)(2,1)}), bf16[8192,256]{0,1:T(8,128)(2,1)}) %all-gather.2.cloned.1.call-update) | async-done | bytes 4194320 | tf_op jit(solution)/shard_map/all_gather | solution.py:13
  204.6 96.6 %conditional.1 = (f32[1,2,512]{2,1,0:T(2,128)S(1)}, f32[1,2,512,128]{3,2,1,0:T(8,128)}) conditional(s32[]{:T(128)} %convert_element_type.47, (bf16[8192,256]{0,1:T(8,128)(2,1)}, s32[8192]{0:T(1024)S(1)}, s32[16,512]{1,0:T(8,128)S(1)}, s32[16,512]{1,0:T(8,128)S(1)}, s32[512]{0:T(512)S(1)}, /*index=5*/s32[512]{0:T(512)S(1)}, ...), branch_computations={%region_3.8_spmd, %region_8.9_spmd} | conditional | flops 276453376 | bytes 26461452 | solution.py:135
  204.6 6.4 %copy.9 = bf16[8192,256]{1,0:T(8,128)(2,1)} copy(bf16[8192,256]{0,1:T(8,128)(2,1)} %get-tuple-element.134) | data formatting | bytes 8388608 | tf_op jit(solution)/shard_map
  211.1 4.4 %fusion.42 = (bf16[8192,128]{1,0:T(8,128)(2,1)}, bf16[8192,128]{1,0:T(8,128)(2,1)}) fusion(bf16[8192,256]{1,0:T(8,128)(2,1)} %copy.9), kind=kLoop, calls=%fused_computation.71 | loop fusion | bytes 8388608 | tf_op jit(solution)/shard_map/split | solution.py:14
  216.4 84.8 %while.14 = (s32[]{:T(128)}, f32[1,2,512]{2,1,0:T(2,128)S(1)}, f32[1,2,512]{2,1,0:T(2,128)S(1)}, f32[1,2,512,128]{3,2,1,0:T(8,128)}, s32[16,512]{1,0:T(8,128)S(1...) while((s32[]{:T(128)}, f32[1,2,512]{2,1,0:T(2,128)S(1)}, ...), condition=%wide.region_7.7_spmd.clone, body=%wide.region_4.6_spmd.clone.sunk | while | flops 276436992 | bytes 8995981 | solution.py:133
  223.4 2.8 fusion.61
  228.7 2.8 fusion.61
  234.1 2.8 fusion.61
  239.4 2.8 fusion.61
  244.7 2.8 fusion.61
  250.0 2.8 fusion.61
  255.3 2.8 fusion.61
  260.6 2.8 fusion.61
  265.9 2.8 fusion.61
  271.2 2.8 fusion.61
  276.6 2.8 fusion.61
  281.9 2.8 fusion.61
  287.2 2.8 fusion.61
  (151 shorter events, 60.3 us)
Async XLA Ops:
  6.5 108.1 %copy-start = (bf16[4096,128]{1,0:T(8,128)(2,1)S(1)}, bf16[4096,128]{1,0:T(8,128)(2,1)}, u32[]{:S(2)}) copy-start(bf16[4096,128]{1,0:T(8,128)(2,1)} %param.13) | copy-start | bytes 3145732
  12.3 102.3 %all-to-all-start = ((bf16[8,64,4096]{2,1,0:T(8,128)(2,1)}), bf16[8,64,4096]{2,1,0:T(8,128)(2,1)}, u32[]{:S(2)}, u32[]{:S(2)}) async-start(bf16[8,64,4096]{2,1,0:T(8,128)(2,1)} %stack.2), calls=%async_computation | async-start | bytes 8388608 | tf_op jit(solution)/shard_map/all_to_all | solution.py:60
  22.6 182.1 %all-gather.2.cloned.1.call-start = ((), (), s32[]{:S(2)}) async-start(), calls=%async_computation.1 | async-start | bytes 4456448 | tf_op jit(solution)/shard_map/all_gather | solution.py:13
  114.6 3.8 %copy-start.2 = (bf16[4096,128]{1,0:T(8,128)(2,1)S(1)}, bf16[4096,128]{1,0:T(8,128)(2,1)}, u32[]{:S(2)}) copy-start(bf16[4096,128]{1,0:T(8,128)(2,1)} %param.14) | copy-start | bytes 3145732
  118.4 5.8 %copy-start.1 = (bf16[4096,256]{1,0:T(8,128)(2,1)S(1)}, bf16[4096,256]{1,0:T(8,128)(2,1)}, u32[]{:S(2)}) copy-start(bf16[4096,256]{1,0:T(8,128)(2,1)} %param.12) | copy-start | bytes 6291460
  124.3 2.9 copy-start.3
Sparse Core Ops, SparseCore 0:
  123.7 80.8 all-gather.1
